TPU v7x, 32 devices: a whole 2x2x4 slice. The times are simulated.
32 devices in a mesh: clips: 2 (over y), ha: 4 (over z), wa: 2 (over core), ta: 2 (over x).
Axes of the slice: x: 2, y: 2, z: 4, core: 2. Of those that a mesh axis runs over, the one named last changes fastest.
Arguments:
- frames: bfloat16 [8, 16, 256, 128], P(('clips', 'ta'), 'ha', 'wa'), parts along dimension 0, may hold values from -12 to 12
- past_first: bfloat16 [4, 16, 256, 128], P('clips', 'ha', 'wa'), parts along dimension 0, may hold values from -6 to 6
- past_second: bfloat16 [4, 16, 256, 128], P('clips', 'ha', 'wa'), parts along dimension 0, may hold values from -6 to 6
- gain_first: float32 [128], replicated, may hold values from 0.5 to 1.5
- shift_first: float32 [128], replicated, may hold values from -3 to 3
- kernel_first: bfloat16 [3, 3, 3, 128, 128], replicated, may hold values from -0.109375 to 0.109375
- bias_first: float32 [128], replicated, may hold values from -2 to 2
- gain_second: float32 [128], replicated, may hold values from 0.5 to 1.5
- shift_second: float32 [128], replicated, may hold values from -3 to 3
- kernel_second: bfloat16 [3, 3, 3, 128, 128], replicated, may hold values from -0.109375 to 0.109375
- bias_second: float32 [128], replicated, may hold values from -2 to 2
Outputs:
- decoded: bfloat16 [8, 16, 256, 128], P(('clips', 'ta'), 'ha', 'wa'), parts along dimension 0
There are 2 independent parts, one for each index of `clips`. A program takes and returns all parts, laid end to end along the dimension named above; an argument that names none is the same for every part. Nothing has to cross between parts.
All inputs are finite; a program needn't handle non-finite values.
Results may differ from a plain program's by a relative error of at most 0.0039.
Values may be sent and summed in bfloat16 or wider, within the bound.
No kernel may reach another device: no remote copies, remote signals or barrier semaphores. Data moves between devices by JAX's collectives and lax.ppermute only.
A program may use at most 64 MiB of HBM per device.

v0:
```python
import jax
import jax.numpy as jnp
from jax import lax
from jax.sharding import PartitionSpec as P

G = 32


EPS = 1e-06


def shifted(value, axis, steps):
    count = lax.axis_size(axis)
    initial, last = (max(0, -steps), min(count, count - steps))
    return lax.ppermute(value, axis, [(source, source + steps) for source in range(initial, last)])


def extended(block, sides, width):
    for axis, dim in sides:
        count = lax.axis_size(axis)
        forward = [(i, i + 1) for i in range(count - 1)]
        backward = [(target, source) for source, target in forward]
        low = lax.ppermute(
            lax.slice_in_dim(block, block.shape[dim] - width, None, axis=dim), axis, forward
        )
        high = lax.ppermute(lax.slice_in_dim(block, 0, width, axis=dim), axis, backward)
        block = jnp.concatenate([low, block, high], axis=dim)
    return block


def group_sums(value):
    nframe, rows, cols, chans = value.shape
    grouped = value.reshape(nframe, rows, cols, G, chans // G)
    return (jnp.sum(grouped, axis=(0, 1, 2, 4)), jnp.sum(grouped * grouped, axis=(0, 1, 2, 4)))


def apply_norm(value, totals, squares, count, gain, shift):
    chans = value.shape[3]
    mean = totals / count
    inverse = lax.rsqrt(squares / count - mean * mean + EPS)
    mean_chan = jnp.repeat(mean, chans // G)
    inverse_chan = jnp.repeat(inverse, chans // G)
    return jax.nn.silu((value - mean_chan) * inverse_chan * gain + shift)


def conv_block(padded, kernel, bias, nframe):
    out_rows = padded.shape[1] - 2
    out_cols = padded.shape[2] - 2
    chans = padded.shape[3]
    stacked = kernel.reshape(3, 3, 3 * chans, chans)
    total = jnp.zeros((nframe * out_rows * out_cols, chans), jnp.float32) + bias
    for time_step in range(3):
        for row_step in range(3):
            slab = jnp.concatenate(
                [
                    padded[
                        time_step : time_step + nframe,
                        row_step : row_step + out_rows,
                        col_step : col_step + out_cols,
                        :,
                    ]
                    for col_step in range(3)
                ],
                axis=3,
            )
            total = total + jnp.dot(
                slab.reshape(nframe * out_rows * out_cols, 3 * chans),
                stacked[time_step, row_step],
                preferred_element_type=jnp.float32,
            )
    return total.reshape(nframe, out_rows, out_cols, chans)


def on_device(
    frames,
    past_first,
    past_second,
    gain_first,
    shift_first,
    kernel_first,
    bias_first,
    gain_second,
    shift_second,
    kernel_second,
    bias_second,
):
    nframe, rows, cols, chans = frames.shape
    count = float(
        nframe
        * rows
        * cols
        * (chans // G)
        * lax.axis_size("ha")
        * lax.axis_size("wa")
        * lax.axis_size("ta")
    )
    source = frames.astype(jnp.float32)
    first_sum, first_square = group_sums(source)
    first_sum, first_square = lax.psum((first_sum, first_square), ("ha", "wa", "ta"))
    act_one = apply_norm(source, first_sum, first_square, count, gain_first, shift_first).astype(
        jnp.bfloat16
    )
    first_time = lax.axis_index("ta") == 0
    carried = shifted(act_one, "ta", 1)
    carried = jnp.where(first_time, past_first, carried)
    joined = jnp.concatenate([carried, act_one], axis=0)
    padded = extended(joined, (("ha", 1), ("wa", 2)), 1)
    hidden = conv_block(padded, kernel_first, bias_first, nframe)
    second_sum, second_square = group_sums(hidden)
    second_sum, second_square = lax.psum((second_sum, second_square), ("ha", "wa", "ta"))
    act_two = apply_norm(
        hidden, second_sum, second_square, count, gain_second, shift_second
    ).astype(jnp.bfloat16)
    carried_two = shifted(act_two, "ta", 1)
    carried_two = jnp.where(first_time, past_second, carried_two)
    joined_two = jnp.concatenate([carried_two, act_two], axis=0)
    padded_two = extended(joined_two, (("ha", 1), ("wa", 2)), 1)
    result = conv_block(padded_two, kernel_second, bias_second, nframe) + source
    return result.astype(jnp.bfloat16)


def solution(mesh):
    return jax.shard_map(
        on_device,
        mesh=mesh,
        in_specs=(
            P(("clips", "ta"), "ha", "wa", None),
            P("clips", "ha", "wa", None),
            P("clips", "ha", "wa", None),
            P(),
            P(),
            P(),
            P(),
            P(),
            P(),
            P(),
            P(),
        ),
        out_specs=P(("clips", "ta"), "ha", "wa", None),
        check_vma=False,
    )
```

profile of v0, /device:TPU:0, one launch (start us, length us, event | category | flops | bytes accessed | tf_op | source)
XLA Modules:
  0.0 123.0 jit_solution(2695239375369031097)
XLA Ops:
  0.0 1.1 convert_reduce_fusion
  1.4 0.1 reduce_sum.51
  1.5 0.1 reduce_sum.54
  1.6 34.9 %all-reduce.1 = (f32[32]{0:T(128)S(1)}, f32[32]{0:T(128)S(1)}) all-reduce(f32[32]{0:T(128)S(1)} %reduce_sum.54, f32[32]{0:T(128)S(1)} %reduce_sum.51), channel_id=1, replica_groups=mesh['clips'=2,'ha'=4,'wa'=2,'ta'=2] {'ha','wa','ta'}, use_global_device_ids=true, to_apply=%region_5.6 | all-reduce | flops 64 | bytes 512 | tf_op jit(solution)/shard_map/psum | solution.py:99
  36.6 0.1 sub.26
  36.8 0.1 mul.59
  36.9 1.2 fusion.12
  38.1 1.3 %collective-permute-start = (bf16[2,4,128,128]{3,2,1,0:T(8,128)(2,1)S(1)}, bf16[2,4,128,128]{3,2,1,0:T(8,128)(2,1)S(1)}, u32[]{:S(2)}, u32[]{:S(2)}) collective-permute-start(bf16[2,4,128,128]{3,2,1,0:T(8,128)(2,1)S(1)} %fusion.12), channel_id=1, source_target_pairs={{0,1},{2,3},{4,5},{6,7},{8,9},{10,11},{12,13},{14,15},{16,17},{18,... | collective-permute-start | bytes 786440 | tf_op jit(solution)/shard_map/ppermute | solution.py:15
  39.4 4.0 %collective-permute-done = bf16[2,4,128,128]{3,2,1,0:T(8,128)(2,1)S(1)} collective-permute-done((bf16[2,4,128,128]{3,2,1,0:T(8,128)(2,1)S(1)}, bf16[2,4,128,128]{3,2,1,0:T(8,128)(2,1)S(1)}, u32[]{:S(2)}, u32[]{:S(2)}) %collective-permute-start) | collective-permute-done | bytes 262176 | tf_op jit(solution)/shard_map/ppermute | solution.py:15
  43.4 1.3 %collective-permute-start.1 = (bf16[4,1,128,128]{3,2,1,0:T(8,128)(2,1)S(1)}, bf16[4,1,128,128]{3,2,1,0:T(8,128)(2,1)S(1)}, u32[]{:S(2)}, u32[]{:S(2)}) collective-permute-start(bf16[4,1,128,128]{3,2,1,0:T(8,128)(2,1)S(1)} %get-tuple-element.75), channel_id=1, source_target_pairs={{0,4},{4,8},{8,12},{1,5},{5,9},{9,13},{2,6},{6,10},{10,14},{3,7},{... | collective-permute-start | bytes 393224 | tf_op jit(solution)/shard_map/ppermute | solution.py:23
  44.7 1.3 %collective-permute-start.2 = (bf16[4,1,128,128]{3,2,1,0:T(8,128)(2,1)S(1)}, bf16[4,1,128,128]{3,2,1,0:T(8,128)(2,1)S(1)}, u32[]{:S(2)}, u32[]{:S(2)}) collective-permute-start(bf16[4,1,128,128]{3,2,1,0:T(8,128)(2,1)S(1)} %get-tuple-element.76), channel_id=1, source_target_pairs={{4,0},{8,4},{12,8},{5,1},{9,5},{13,9},{6,2},{10,6},{14,10},{7,3},{... | collective-permute-start | bytes 393224 | tf_op jit(solution)/shard_map/ppermute | solution.py:26
  46.0 1.2 collective-permute-done.1
  47.2 4.4 %collective-permute-done.2 = bf16[4,1,128,128]{3,2,1,0:T(8,128)(2,1)S(1)} collective-permute-done((bf16[4,1,128,128]{3,2,1,0:T(8,128)(2,1)S(1)}, bf16[4,1,128,128]{3,2,1,0:T(8,128)(2,1)S(1)}, u32[]{:S(2)}, u32[]{:S(2)}) %collective-permute-start.2) | collective-permute-done | bytes 131104 | tf_op jit(solution)/shard_map/ppermute | solution.py:26
  51.6 1.3 %collective-permute-start.3 = (bf16[4,6,1,128]{3,2,1,0:T(2,128)(2,1)S(1)}, bf16[4,6,1,128]{3,2,1,0:T(2,128)(2,1)S(1)}, u32[]{:S(2)}, u32[]{:S(2)}) collective-permute-start(bf16[4,6,1,128]{3,2,1,0:T(2,128)(2,1)S(1)} %get-tuple-element.55), channel_id=1, source_target_pairs={{0,2},{1,3},{4,6},{5,7},{8,10},{9,11},{12,14},{13,15},{16,18},{17,... | collective-permute-start | bytes 18440 | tf_op jit(solution)/shard_map/ppermute | solution.py:23
  52.9 1.3 %collective-permute-start.4 = (bf16[4,6,1,128]{3,2,1,0:T(2,128)(2,1)S(1)}, bf16[4,6,1,128]{3,2,1,0:T(2,128)(2,1)S(1)}, u32[]{:S(2)}, u32[]{:S(2)}) collective-permute-start(bf16[4,6,1,128]{3,2,1,0:T(2,128)(2,1)S(1)} %get-tuple-element.56), channel_id=1, source_target_pairs={{2,0},{3,1},{6,4},{7,5},{10,8},{11,9},{14,12},{15,13},{18,16},{19,... | collective-permute-start | bytes 18440 | tf_op jit(solution)/shard_map/ppermute | solution.py:26
  54.3 0.3 fusion.22
  54.6 1.3 %collective-permute-done.4 = bf16[4,6,1,128]{3,2,1,0:T(2,128)(2,1)S(1)} collective-permute-done((bf16[4,6,1,128]{3,2,1,0:T(2,128)(2,1)S(1)}, bf16[4,6,1,128]{3,2,1,0:T(2,128)(2,1)S(1)}, u32[]{:S(2)}, u32[]{:S(2)}) %collective-permute-start.4) | collective-permute-done | bytes 6176 | tf_op jit(solution)/shard_map/ppermute | solution.py:26
  56.0 0.5 maximum_maximum_fusion
  56.4 1.0 fusion.18
  57.6 1.0 copy-done.1
  58.6 0.4 convolution_add_fusion.17
  59.0 0.4 pad_maximum_fusion.10
  59.3 0.4 convolution_add_fusion.16
  59.8 0.4 convolution_add_fusion.15
  60.3 0.4 convolution_add_fusion.14
  60.7 0.4 convolution_add_fusion.13
  61.2 0.4 convolution_add_fusion.12
  61.7 0.4 convolution_add_fusion.11
  62.1 0.4 convolution_add_fusion.10
  62.6 0.4 fusion.15
  63.1 0.1 reduce_sum.72
  63.3 0.1 reduce_sum.75
  63.4 32.6 %all-reduce = (f32[32]{0:T(128)S(1)}, f32[32]{0:T(128)S(1)}) all-reduce(f32[32]{0:T(128)S(1)} %reduce_sum.75, f32[32]{0:T(128)S(1)} %reduce_sum.72), channel_id=1, replica_groups=mesh['clips'=2,'ha'=4,'wa'=2,'ta'=2] {'ha','wa','ta'}, use_global_device_ids=true, to_apply=%region_11.12 | all-reduce | flops 64 | bytes 512 | tf_op jit(solution)/shard_map/psum | solution.py:110
  96.2 0.1 sub.30
  96.3 0.1 mul.67
  96.5 0.2 multiply_convert_fusion
  96.7 1.3 %collective-permute-start.5 = (bf16[2,4,128,128]{3,2,1,0:T(8,128)(2,1)S(1)}, bf16[2,4,128,128]{3,2,1,0:T(8,128)(2,1)S(1)}, u32[]{:S(2)}, u32[]{:S(2)}) collective-permute-start(bf16[2,4,128,128]{3,2,1,0:T(8,128)(2,1)S(1)} %multiply_convert_fusion), channel_id=1, source_target_pairs={{0,1},{2,3},{4,5},{6,7},{8,9},{10,11},{12,13},{14,15},{16,17},{18,... | collective-permute-start | bytes 786440 | tf_op jit(solution)/shard_map/ppermute | solution.py:15
  98.0 4.0 %collective-permute-done.5 = bf16[2,4,128,128]{3,2,1,0:T(8,128)(2,1)S(1)} collective-permute-done((bf16[2,4,128,128]{3,2,1,0:T(8,128)(2,1)S(1)}, bf16[2,4,128,128]{3,2,1,0:T(8,128)(2,1)S(1)}, u32[]{:S(2)}, u32[]{:S(2)}) %collective-permute-start.5) | collective-permute-done | bytes 262176 | tf_op jit(solution)/shard_map/ppermute | solution.py:15
  102.0 1.3 %collective-permute-start.6 = (bf16[4,1,128,128]{3,2,1,0:T(8,128)(2,1)S(1)}, bf16[4,1,128,128]{3,2,1,0:T(8,128)(2,1)S(1)}, u32[]{:S(2)}, u32[]{:S(2)}) collective-permute-start(bf16[4,1,128,128]{3,2,1,0:T(8,128)(2,1)S(1)} %get-tuple-element.71), channel_id=1, source_target_pairs={{0,4},{4,8},{8,12},{1,5},{5,9},{9,13},{2,6},{6,10},{10,14},{3,7},{... | collective-permute-start | bytes 393224 | tf_op jit(solution)/shard_map/ppermute | solution.py:23
  103.3 1.3 %collective-permute-start.7 = (bf16[4,1,128,128]{3,2,1,0:T(8,128)(2,1)S(1)}, bf16[4,1,128,128]{3,2,1,0:T(8,128)(2,1)S(1)}, u32[]{:S(2)}, u32[]{:S(2)}) collective-permute-start(bf16[4,1,128,128]{3,2,1,0:T(8,128)(2,1)S(1)} %get-tuple-element.72), channel_id=1, source_target_pairs={{4,0},{8,4},{12,8},{5,1},{9,5},{13,9},{6,2},{10,6},{14,10},{7,3},{... | collective-permute-start | bytes 393224 | tf_op jit(solution)/shard_map/ppermute | solution.py:26
  104.6 1.2 collective-permute-done.6
  105.8 4.4 %collective-permute-done.7 = bf16[4,1,128,128]{3,2,1,0:T(8,128)(2,1)S(1)} collective-permute-done((bf16[4,1,128,128]{3,2,1,0:T(8,128)(2,1)S(1)}, bf16[4,1,128,128]{3,2,1,0:T(8,128)(2,1)S(1)}, u32[]{:S(2)}, u32[]{:S(2)}) %collective-permute-start.7) | collective-permute-done | bytes 131104 | tf_op jit(solution)/shard_map/ppermute | solution.py:26
  110.2 1.3 %collective-permute-start.8 = (bf16[4,6,1,128]{3,2,1,0:T(2,128)(2,1)S(1)}, bf16[4,6,1,128]{3,2,1,0:T(2,128)(2,1)S(1)}, u32[]{:S(2)}, u32[]{:S(2)}) collective-permute-start(bf16[4,6,1,128]{3,2,1,0:T(2,128)(2,1)S(1)} %get-tuple-element.51), channel_id=1, source_target_pairs={{0,2},{1,3},{4,6},{5,7},{8,10},{9,11},{12,14},{13,15},{16,18},{17,... | collective-permute-start | bytes 18440 | tf_op jit(solution)/shard_map/ppermute | solution.py:23
  111.5 1.5 %collective-permute-start.9 = (bf16[4,6,1,128]{3,2,1,0:T(2,128)(2,1)S(1)}, bf16[4,6,1,128]{3,2,1,0:T(2,128)(2,1)S(1)}, u32[]{:S(2)}, u32[]{:S(2)}) collective-permute-start(bf16[4,6,1,128]{3,2,1,0:T(2,128)(2,1)S(1)} %get-tuple-element.52), channel_id=1, source_target_pairs={{2,0},{3,1},{6,4},{7,5},{10,8},{11,9},{14,12},{15,13},{18,16},{19,... | collective-permute-start | bytes 18440 | tf_op jit(solution)/shard_map/ppermute | solution.py:26
  113.1 0.1 fusion.20
  113.2 0.1 fusion.21
  113.4 1.2 collective-permute-done.9
  114.6 0.5 maximum_maximum_fusion.1
  115.0 0.6 fusion.16
  115.6 0.6 fusion.17
  116.2 0.1 pad_maximum_fusion.12
  116.3 1.0 copy-done.2
  117.4 0.4 convolution_add_fusion.8
  117.8 0.4 pad_maximum_fusion.18
  118.1 0.4 convolution_add_fusion.7
  118.6 0.4 convolution_add_fusion.6
  119.1 0.4 convolution_add_fusion.5
  119.5 0.4 convolution_add_fusion.4
  120.0 0.4 convolution_add_fusion.3
  120.5 0.4 convolution_add_fusion.2
  120.8 0.4 convolution_add_fusion.1
  121.3 0.4 convolution_add_fusion
  121.7 0.6 copy-done
  122.3 0.8 fusion.14
  (46 shorter events, 2.3 us)
Async XLA Ops:
  0.0 43.4 %copy-start.3 = (bf16[2,4,128,128]{3,2,1,0:T(8,128)(2,1)S(1)}, bf16[2,4,128,128]{3,2,1,0:T(8,128)(2,1)}, u32[]{:S(2)}) copy-start(bf16[2,4,128,128]{3,2,1,0:T(8,128)(2,1)} %param.12) | copy-start | bytes 786436
  38.1 5.3 %collective-permute-start = (bf16[2,4,128,128]{3,2,1,0:T(8,128)(2,1)S(1)}, bf16[2,4,128,128]{3,2,1,0:T(8,128)(2,1)S(1)}, u32[]{:S(2)}, u32[]{:S(2)}) collective-permute-start(bf16[2,4,128,128]{3,2,1,0:T(8,128)(2,1)S(1)} %fusion.12), channel_id=1, source_target_pairs={{0,1},{2,3},{4,5},{6,7},{8,9},{10,11},{12,13},{14,15},{16,17},{18,... | collective-permute-start | bytes 786440 | tf_op jit(solution)/shard_map/ppermute | solution.py:15
  43.4 3.8 %collective-permute-start.1 = (bf16[4,1,128,128]{3,2,1,0:T(8,128)(2,1)S(1)}, bf16[4,1,128,128]{3,2,1,0:T(8,128)(2,1)S(1)}, u32[]{:S(2)}, u32[]{:S(2)}) collective-permute-start(bf16[4,1,128,128]{3,2,1,0:T(8,128)(2,1)S(1)} %get-tuple-element.75), channel_id=1, source_target_pairs={{0,4},{4,8},{8,12},{1,5},{5,9},{9,13},{2,6},{6,10},{10,14},{3,7},{... | collective-permute-start | bytes 393224 | tf_op jit(solution)/shard_map/ppermute | solution.py:23
  44.7 6.9 %collective-permute-start.2 = (bf16[4,1,128,128]{3,2,1,0:T(8,128)(2,1)S(1)}, bf16[4,1,128,128]{3,2,1,0:T(8,128)(2,1)S(1)}, u32[]{:S(2)}, u32[]{:S(2)}) collective-permute-start(bf16[4,1,128,128]{3,2,1,0:T(8,128)(2,1)S(1)} %get-tuple-element.76), channel_id=1, source_target_pairs={{4,0},{8,4},{12,8},{5,1},{9,5},{13,9},{6,2},{10,6},{14,10},{7,3},{... | collective-permute-start | bytes 393224 | tf_op jit(solution)/shard_map/ppermute | solution.py:26
  51.6 3.0 %collective-permute-start.3 = (bf16[4,6,1,128]{3,2,1,0:T(2,128)(2,1)S(1)}, bf16[4,6,1,128]{3,2,1,0:T(2,128)(2,1)S(1)}, u32[]{:S(2)}, u32[]{:S(2)}) collective-permute-start(bf16[4,6,1,128]{3,2,1,0:T(2,128)(2,1)S(1)} %get-tuple-element.55), channel_id=1, source_target_pairs={{0,2},{1,3},{4,6},{5,7},{8,10},{9,11},{12,14},{13,15},{16,18},{17,... | collective-permute-start | bytes 18440 | tf_op jit(solution)/shard_map/ppermute | solution.py:23
  52.9 3.1 %collective-permute-start.4 = (bf16[4,6,1,128]{3,2,1,0:T(2,128)(2,1)S(1)}, bf16[4,6,1,128]{3,2,1,0:T(2,128)(2,1)S(1)}, u32[]{:S(2)}, u32[]{:S(2)}) collective-permute-start(bf16[4,6,1,128]{3,2,1,0:T(2,128)(2,1)S(1)} %get-tuple-element.56), channel_id=1, source_target_pairs={{2,0},{3,1},{6,4},{7,5},{10,8},{11,9},{14,12},{15,13},{18,16},{19,... | collective-permute-start | bytes 18440 | tf_op jit(solution)/shard_map/ppermute | solution.py:26
  57.4 1.2 copy-start.1
  57.4 1.2 copy-start.5
  62.5 33.9 %copy-start.7 = (f32[128]{0:T(128)S(1)}, f32[128]{0:T(128)}, u32[]{:S(2)}) copy-start(f32[128]{0:T(128)} %param.19) | copy-start | bytes 1540
  62.6 33.9 %copy-start.8 = (f32[128]{0:T(128)S(1)}, f32[128]{0:T(128)}, u32[]{:S(2)}) copy-start(f32[128]{0:T(128)} %param.18) | copy-start | bytes 1540
  63.0 39.0 %copy-start.4 = (bf16[2,4,128,128]{3,2,1,0:T(8,128)(2,1)S(1)}, bf16[2,4,128,128]{3,2,1,0:T(8,128)(2,1)}, u32[]{:S(2)}) copy-start(bf16[2,4,128,128]{3,2,1,0:T(8,128)(2,1)} %param.13) | copy-start | bytes 786436
  96.7 5.3 %collective-permute-start.5 = (bf16[2,4,128,128]{3,2,1,0:T(8,128)(2,1)S(1)}, bf16[2,4,128,128]{3,2,1,0:T(8,128)(2,1)S(1)}, u32[]{:S(2)}, u32[]{:S(2)}) collective-permute-start(bf16[2,4,128,128]{3,2,1,0:T(8,128)(2,1)S(1)} %multiply_convert_fusion), channel_id=1, source_target_pairs={{0,1},{2,3},{4,5},{6,7},{8,9},{10,11},{12,13},{14,15},{16,17},{18,... | collective-permute-start | bytes 786440 | tf_op jit(solution)/shard_map/ppermute | solution.py:15
  102.0 3.8 %collective-permute-start.6 = (bf16[4,1,128,128]{3,2,1,0:T(8,128)(2,1)S(1)}, bf16[4,1,128,128]{3,2,1,0:T(8,128)(2,1)S(1)}, u32[]{:S(2)}, u32[]{:S(2)}) collective-permute-start(bf16[4,1,128,128]{3,2,1,0:T(8,128)(2,1)S(1)} %get-tuple-element.71), channel_id=1, source_target_pairs={{0,4},{4,8},{8,12},{1,5},{5,9},{9,13},{2,6},{6,10},{10,14},{3,7},{... | collective-permute-start | bytes 393224 | tf_op jit(solution)/shard_map/ppermute | solution.py:23
  103.3 6.9 %collective-permute-start.7 = (bf16[4,1,128,128]{3,2,1,0:T(8,128)(2,1)S(1)}, bf16[4,1,128,128]{3,2,1,0:T(8,128)(2,1)S(1)}, u32[]{:S(2)}, u32[]{:S(2)}) collective-permute-start(bf16[4,1,128,128]{3,2,1,0:T(8,128)(2,1)S(1)} %get-tuple-element.72), channel_id=1, source_target_pairs={{4,0},{8,4},{12,8},{5,1},{9,5},{13,9},{6,2},{10,6},{14,10},{7,3},{... | collective-permute-start | bytes 393224 | tf_op jit(solution)/shard_map/ppermute | solution.py:26
  110.2 3.2 %collective-permute-start.8 = (bf16[4,6,1,128]{3,2,1,0:T(2,128)(2,1)S(1)}, bf16[4,6,1,128]{3,2,1,0:T(2,128)(2,1)S(1)}, u32[]{:S(2)}, u32[]{:S(2)}) collective-permute-start(bf16[4,6,1,128]{3,2,1,0:T(2,128)(2,1)S(1)} %get-tuple-element.51), channel_id=1, source_target_pairs={{0,2},{1,3},{4,6},{5,7},{8,10},{9,11},{12,14},{13,15},{16,18},{17,... | collective-permute-start | bytes 18440 | tf_op jit(solution)/shard_map/ppermute | solution.py:23
  111.5 3.1 %collective-permute-start.9 = (bf16[4,6,1,128]{3,2,1,0:T(2,128)(2,1)S(1)}, bf16[4,6,1,128]{3,2,1,0:T(2,128)(2,1)S(1)}, u32[]{:S(2)}, u32[]{:S(2)}) collective-permute-start(bf16[4,6,1,128]{3,2,1,0:T(2,128)(2,1)S(1)} %get-tuple-element.52), channel_id=1, source_target_pairs={{2,0},{3,1},{6,4},{7,5},{10,8},{11,9},{14,12},{15,13},{18,16},{19,... | collective-permute-start | bytes 18440 | tf_op jit(solution)/shard_map/ppermute | solution.py:26
  116.2 1.2 copy-start.2
  116.2 1.2 copy-start.6
  121.3 1.0 copy-start
where the time goes:
time: 124 us; the launch traced here: 123 us
  blocking collectives  67.6 us (55%)
  waiting for transfers between devices  21.6 us (17%)
  starting transfers between devices  13.1 us (11%)
  other arithmetic  7.01 us (6%)
  matrix products  6.64 us (5%)
  local copies, waits for them, and re-layouts  6.49 us (5%)
    psum x1, blocking collectives, on_device(): lax.psum((first_sum, first_square), ('ha', 'wa', 'ta'))  34.9 us
    psum x1, blocking collectives, on_device(): lax.psum((second_sum, second_square), ('ha', 'wa', 'ta'))  32.6 us
    ppermute x4, waiting for transfers between devices, extended(): lax.ppermute(lax.slice_in_dim(block, 0, width, axis=dim), axis, backward)  11.3 us
    ppermute x2, waiting for transfers between devices, shifted(): lax.ppermute(value, axis, [(source, source + steps) for source in range(i...  7.93 us
    dot_general x18, matrix products, conv_block(): jnp.dot(slab.reshape(nframe * out_rows * out_cols, 3 * chans), stacked[ti...  6.64 us
    ppermute x4, starting transfers between devices, extended(): lax.ppermute(lax.slice_in_dim(block, 0, width, axis=dim), axis, backward)  5.35 us
    ppermute x4, starting transfers between devices, extended(): lax.ppermute(lax.slice_in_dim(block, block.shape[dim] - width, None, axis...  5.18 us
    slice x6, local copies, waits for them, and re-layouts, conv_block(): padded[time_step:time_step + nframe, row_step:row_step + out_rows, col_st...  2.71 us
  transfers between devices with their start and end apart: 10, of which 8 were waited for; matrix products, arithmetic and copies ran while one was open for 1% of the time, Pallas kernels for 0%

commit v1 on v0

--- a/solution.py
+++ b/solution.py
@@ -26,6 +26,17 @@
         high = lax.ppermute(lax.slice_in_dim(block, 0, width, axis=dim), axis, backward)
         block = jnp.concatenate([low, block, high], axis=dim)
     return block
+
+
+BANDS = ("ha", "wa", "ta")
+
+
+def summed(parts):
+    joined = jnp.concatenate(parts)
+    count = lax.axis_size("ha") * lax.axis_size("wa") * lax.axis_size("ta")
+    spread = jnp.broadcast_to(joined[None], (count, joined.shape[0]))
+    gathered = lax.all_to_all(spread, BANDS, 0, 0, tiled=True)
+    return jnp.split(jnp.sum(gathered, axis=0), len(parts))
 
 
 def group_sums(value):
@@ -96,7 +107,7 @@
     )
     source = frames.astype(jnp.float32)
     first_sum, first_square = group_sums(source)
-    first_sum, first_square = lax.psum((first_sum, first_square), ("ha", "wa", "ta"))
+    first_sum, first_square = summed((first_sum, first_square))
     act_one = apply_norm(source, first_sum, first_square, count, gain_first, shift_first).astype(
         jnp.bfloat16
     )
@@ -107,7 +118,7 @@
     padded = extended(joined, (("ha", 1), ("wa", 2)), 1)
     hidden = conv_block(padded, kernel_first, bias_first, nframe)
     second_sum, second_square = group_sums(hidden)
-    second_sum, second_square = lax.psum((second_sum, second_square), ("ha", "wa", "ta"))
+    second_sum, second_square = summed((second_sum, second_square))
     act_two = apply_norm(
         hidden, second_sum, second_square, count, gain_second, shift_second
     ).astype(jnp.bfloat16)

time: 124 us -> 87.8 us (0.71)
  blocking collectives: 67.6 us -> 23.7 us
  starting transfers between devices: 13.1 us -> 17.9 us
  waiting for transfers between devices: 21.6 us -> 24.7 us
    psum x2 -> x0, blocking collectives: 67.6 us -> none  [the longest x1 34.9 us: on_device(): lax.psum((first_sum, first_square), ('ha', 'wa', 'ta'))]
    all_to_all x0 -> x2, blocking collectives: none -> 23.7 us  [summed(): gathered = lax.all_to_all(spread, BANDS, 0, 0, tiled=True)]
    ppermute x2, waiting for transfers between devices: 7.93 us -> 11 us  [shifted(): lax.ppermute(value, axis, [(source, source + steps) for source in range(i...]
    ppermute x4, starting transfers between devices: 5.18 us -> 7.55 us  [extended(): lax.ppermute(lax.slice_in_dim(block, block.shape[dim] - width, None, axis...]
    ppermute x2, starting transfers between devices: 2.61 us -> 4.97 us  [shifted(): lax.ppermute(value, axis, [(source, source + steps) for source in range(i...]
where the time goes in v1:
time: 87.8 us; the launch traced here: 87.4 us
  waiting for transfers between devices  24.7 us (28%)
  blocking collectives  23.7 us (27%)
  starting transfers between devices  17.9 us (20%)
  other arithmetic  7.34 us (8%)
  matrix products  6.66 us (8%)
  local copies, waits for them, and re-layouts  6.51 us (7%)
    all_to_all x2, blocking collectives, summed(): gathered = lax.all_to_all(spread, BANDS, 0, 0, tiled=True)  23.7 us
    ppermute x4, waiting for transfers between devices, extended(): lax.ppermute(lax.slice_in_dim(block, 0, width, axis=dim), axis, backward)  11.3 us
    ppermute x2, waiting for transfers between devices, shifted(): lax.ppermute(value, axis, [(source, source + steps) for source in range(i...  11 us
    ppermute x4, starting transfers between devices, extended(): lax.ppermute(lax.slice_in_dim(block, block.shape[dim] - width, None, axis...  7.55 us
    dot_general x18, matrix products, conv_block(): jnp.dot(slab.reshape(nframe * out_rows * out_cols, 3 * chans), stacked[ti...  6.66 us
    ppermute x4, starting transfers between devices, extended(): lax.ppermute(lax.slice_in_dim(block, 0, width, axis=dim), axis, backward)  5.35 us
    ppermute x2, starting transfers between devices, shifted(): lax.ppermute(value, axis, [(source, source + steps) for source in range(i...  4.97 us
    slice x6, local copies, waits for them, and re-layouts, conv_block(): padded[time_step:time_step + nframe, row_step:row_step + out_rows, col_st...  2.71 us
  transfers between devices with their start and end apart: 10, of which 8 were waited for; matrix products, arithmetic and copies ran while one was open for 1% of the time, Pallas kernels for 0%

profile of v1, /device:TPU:0, one launch (start us, length us, event | category | flops | bytes accessed | tf_op | source)
XLA Modules:
  0.0 87.4 jit_solution(6356464519803064452)
XLA Ops:
  0.0 1.1 %convert_reduce_fusion = (f32[128]{0:T(128)S(1)}, f32[128]{0:T(128)S(1)}) fusion(bf16[2,4,128,128]{3,2,1,0:T(8,128)(2,1)} %param.11), kind=kLoop, calls=%fused_computation.21 | loop fusion | flops 524032 | bytes 263168 | tf_op jit(solution)/shard_map/reduce_sum | solution.py:45
  1.4 0.1 reduce_sum.67
  1.5 0.1 reduce_sum.73
  1.7 13.6 %all_to_all.12 = f32[16,1,64]{2,1,0:T(1,128)S(1)} all-to-all(f32[16,1,64]{2,1,0:T(1,128)S(1)} %broadcast_in_dim.12), channel_id=1, replica_groups=mesh['clips'=2,'ha'=4,'wa'=2,'ta'=2] {'ha','wa','ta'}, dimensions={0} | all-to-all | bytes 8192 | tf_op jit(solution)/shard_map/all_to_all | solution.py:38
  15.4 0.1 sub.26
  15.6 0.1 mul.59
  15.7 1.2 %fusion.13 = bf16[2,4,128,128]{3,2,1,0:T(8,128)(2,1)S(1)} fusion(bf16[2,4,128,128]{3,2,1,0:T(8,128)(2,1)} %param.11, f32[128]{0:T(128)} %param.15, f32[128]{0:T(128)} %param.14, f32[128]{0:T(128)S(1)} %mul.59, f32[128]{0:T(128)S(1)} %sub.26), kind=kLoop, calls=%fused_computation.61 | loop fusion | flops 1310720 | bytes 526336 | tf_op jit(solution)/shard_map/convert_element_type | solution.py:111
  16.9 2.5 %collective-permute-start = (bf16[2,4,128,128]{3,2,1,0:T(8,128)(2,1)S(1)}, bf16[2,4,128,128]{3,2,1,0:T(8,128)(2,1)S(1)}, u32[]{:S(2)}, u32[]{:S(2)}) collective-permute-start(bf16[2,4,128,128]{3,2,1,0:T(8,128)(2,1)S(1)} %fusion.13), channel_id=1, source_target_pairs={{0,1},{2,3},{4,5},{6,7},{8,9},{10,11},{12,13},{14,15},{16,17},{18,... | collective-permute-start | bytes 786440 | tf_op jit(solution)/shard_map/ppermute | solution.py:15
  19.4 5.5 %collective-permute-done = bf16[2,4,128,128]{3,2,1,0:T(8,128)(2,1)S(1)} collective-permute-done((bf16[2,4,128,128]{3,2,1,0:T(8,128)(2,1)S(1)}, bf16[2,4,128,128]{3,2,1,0:T(8,128)(2,1)S(1)}, u32[]{:S(2)}, u32[]{:S(2)}) %collective-permute-start) | collective-permute-done | bytes 262176 | tf_op jit(solution)/shard_map/ppermute | solution.py:15
  25.0 2.5 %collective-permute-start.1 = (bf16[4,1,128,128]{3,2,1,0:T(8,128)(2,1)S(1)}, bf16[4,1,128,128]{3,2,1,0:T(8,128)(2,1)S(1)}, u32[]{:S(2)}, u32[]{:S(2)}) collective-permute-start(bf16[4,1,128,128]{3,2,1,0:T(8,128)(2,1)S(1)} %get-tuple-element.71), channel_id=1, source_target_pairs={{0,4},{4,8},{8,12},{1,5},{5,9},{9,13},{2,6},{6,10},{10,14},{3,7},{... | collective-permute-start | bytes 393224 | tf_op jit(solution)/shard_map/ppermute | solution.py:23
  27.5 1.3 %collective-permute-start.2 = (bf16[4,1,128,128]{3,2,1,0:T(8,128)(2,1)S(1)}, bf16[4,1,128,128]{3,2,1,0:T(8,128)(2,1)S(1)}, u32[]{:S(2)}, u32[]{:S(2)}) collective-permute-start(bf16[4,1,128,128]{3,2,1,0:T(8,128)(2,1)S(1)} %get-tuple-element.72), channel_id=1, source_target_pairs={{4,0},{8,4},{12,8},{5,1},{9,5},{13,9},{6,2},{10,6},{14,10},{7,3},{... | collective-permute-start | bytes 393224 | tf_op jit(solution)/shard_map/ppermute | solution.py:26
  28.8 1.2 %collective-permute-done.1 = bf16[4,1,128,128]{3,2,1,0:T(8,128)(2,1)S(1)} collective-permute-done((bf16[4,1,128,128]{3,2,1,0:T(8,128)(2,1)S(1)}, bf16[4,1,128,128]{3,2,1,0:T(8,128)(2,1)S(1)}, u32[]{:S(2)}, u32[]{:S(2)}) %collective-permute-start.1) | collective-permute-done | bytes 131104 | tf_op jit(solution)/shard_map/ppermute | solution.py:23
  30.0 4.4 %collective-permute-done.2 = bf16[4,1,128,128]{3,2,1,0:T(8,128)(2,1)S(1)} collective-permute-done((bf16[4,1,128,128]{3,2,1,0:T(8,128)(2,1)S(1)}, bf16[4,1,128,128]{3,2,1,0:T(8,128)(2,1)S(1)}, u32[]{:S(2)}, u32[]{:S(2)}) %collective-permute-start.2) | collective-permute-done | bytes 131104 | tf_op jit(solution)/shard_map/ppermute | solution.py:26
  34.4 1.3 %collective-permute-start.3 = (bf16[4,6,1,128]{3,2,1,0:T(2,128)(2,1)S(1)}, bf16[4,6,1,128]{3,2,1,0:T(2,128)(2,1)S(1)}, u32[]{:S(2)}, u32[]{:S(2)}) collective-permute-start(bf16[4,6,1,128]{3,2,1,0:T(2,128)(2,1)S(1)} %get-tuple-element.51), channel_id=1, source_target_pairs={{0,2},{1,3},{4,6},{5,7},{8,10},{9,11},{12,14},{13,15},{16,18},{17,... | collective-permute-start | bytes 18440 | tf_op jit(solution)/shard_map/ppermute | solution.py:23
  35.7 1.3 %collective-permute-start.4 = (bf16[4,6,1,128]{3,2,1,0:T(2,128)(2,1)S(1)}, bf16[4,6,1,128]{3,2,1,0:T(2,128)(2,1)S(1)}, u32[]{:S(2)}, u32[]{:S(2)}) collective-permute-start(bf16[4,6,1,128]{3,2,1,0:T(2,128)(2,1)S(1)} %get-tuple-element.52), channel_id=1, source_target_pairs={{2,0},{3,1},{6,4},{7,5},{10,8},{11,9},{14,12},{15,13},{18,16},{19,... | collective-permute-start | bytes 18440 | tf_op jit(solution)/shard_map/ppermute | solution.py:26
  37.1 0.3 fusion.22
  37.4 1.3 %collective-permute-done.4 = bf16[4,6,1,128]{3,2,1,0:T(2,128)(2,1)S(1)} collective-permute-done((bf16[4,6,1,128]{3,2,1,0:T(2,128)(2,1)S(1)}, bf16[4,6,1,128]{3,2,1,0:T(2,128)(2,1)S(1)}, u32[]{:S(2)}, u32[]{:S(2)}) %collective-permute-start.4) | collective-permute-done | bytes 6176 | tf_op jit(solution)/shard_map/ppermute | solution.py:26
  38.7 0.5 maximum_maximum_fusion
  39.2 1.0 %fusion.18 = (bf16[2,4,128,128]{3,2,1,0:T(8,128)(2,1)S(1)}, bf16[2,4,128,128]{3,2,1,0:T(8,128)(2,1)S(1)}, bf16[2,4,128,128]{3,2,1,0:T(8,128)(2,1)S(1)}, bf16[2,4...) fusion(bf16[4,6,129,128]{3,2,1,0:T(8,128)(2,1)S(1)} %get-tuple-, ...), kind=kLoop, calls=%fused_computation.106 | loop fusion | bytes 9437184 | tf_op jit(solution)/shard_map/slice | solution.py:67
  40.3 1.0 %copy-done.1 = bf16[3,3,3,128,128]{4,3,2,1,0:T(8,128)(2,1)S(1)} copy-done((bf16[3,3,3,128,128]{4,3,2,1,0:T(8,128)(2,1)S(1)}, bf16[3,3,3,128,128]{4,3,2,1,0:T(8,128)(2,1)}, u32[]{:S(2)}) %copy-start.1) | copy-done | bytes 884760
  41.4 0.4 convolution_add_fusion.17
  41.7 0.4 pad_maximum_fusion.10
  42.1 0.4 convolution_add_fusion.16
  42.6 0.4 convolution_add_fusion.15
  43.1 0.4 convolution_add_fusion.14
  43.5 0.4 convolution_add_fusion.13
  43.9 0.4 convolution_add_fusion.12
  44.4 0.4 convolution_add_fusion.11
  44.8 0.4 convolution_add_fusion.10
  45.3 0.4 fusion.15
  45.9 0.1 reduce_sum.91
  46.1 0.1 reduce_sum.94
  46.3 10.1 %all_to_all.13 = f32[16,1,64]{2,1,0:T(1,128)S(1)} all-to-all(f32[16,1,64]{2,1,0:T(1,128)S(1)} %broadcast_in_dim.15), channel_id=1, replica_groups=mesh['clips'=2,'ha'=4,'wa'=2,'ta'=2] {'ha','wa','ta'}, dimensions={0} | all-to-all | bytes 8192 | tf_op jit(solution)/shard_map/all_to_all | solution.py:38
  56.5 0.1 sub.30
  56.7 0.1 mul.67
  56.9 0.2 multiply_convert_fusion
  57.0 2.5 %collective-permute-start.5 = (bf16[2,4,128,128]{3,2,1,0:T(8,128)(2,1)S(1)}, bf16[2,4,128,128]{3,2,1,0:T(8,128)(2,1)S(1)}, u32[]{:S(2)}, u32[]{:S(2)}) collective-permute-start(bf16[2,4,128,128]{3,2,1,0:T(8,128)(2,1)S(1)} %multiply_convert_fusion), channel_id=1, source_target_pairs={{0,1},{2,3},{4,5},{6,7},{8,9},{10,11},{12,13},{14,15},{16,17},{18,... | collective-permute-start | bytes 786440 | tf_op jit(solution)/shard_map/ppermute | solution.py:15
  59.5 5.5 %collective-permute-done.5 = bf16[2,4,128,128]{3,2,1,0:T(8,128)(2,1)S(1)} collective-permute-done((bf16[2,4,128,128]{3,2,1,0:T(8,128)(2,1)S(1)}, bf16[2,4,128,128]{3,2,1,0:T(8,128)(2,1)S(1)}, u32[]{:S(2)}, u32[]{:S(2)}) %collective-permute-start.5) | collective-permute-done | bytes 262176 | tf_op jit(solution)/shard_map/ppermute | solution.py:15
  65.1 2.5 %collective-permute-start.6 = (bf16[4,1,128,128]{3,2,1,0:T(8,128)(2,1)S(1)}, bf16[4,1,128,128]{3,2,1,0:T(8,128)(2,1)S(1)}, u32[]{:S(2)}, u32[]{:S(2)}) collective-permute-start(bf16[4,1,128,128]{3,2,1,0:T(8,128)(2,1)S(1)} %get-tuple-element.67), channel_id=1, source_target_pairs={{0,4},{4,8},{8,12},{1,5},{5,9},{9,13},{2,6},{6,10},{10,14},{3,7},{... | collective-permute-start | bytes 393224 | tf_op jit(solution)/shard_map/ppermute | solution.py:23
  67.6 1.3 %collective-permute-start.7 = (bf16[4,1,128,128]{3,2,1,0:T(8,128)(2,1)S(1)}, bf16[4,1,128,128]{3,2,1,0:T(8,128)(2,1)S(1)}, u32[]{:S(2)}, u32[]{:S(2)}) collective-permute-start(bf16[4,1,128,128]{3,2,1,0:T(8,128)(2,1)S(1)} %get-tuple-element.68), channel_id=1, source_target_pairs={{4,0},{8,4},{12,8},{5,1},{9,5},{13,9},{6,2},{10,6},{14,10},{7,3},{... | collective-permute-start | bytes 393224 | tf_op jit(solution)/shard_map/ppermute | solution.py:26
  68.9 1.2 %collective-permute-done.6 = bf16[4,1,128,128]{3,2,1,0:T(8,128)(2,1)S(1)} collective-permute-done((bf16[4,1,128,128]{3,2,1,0:T(8,128)(2,1)S(1)}, bf16[4,1,128,128]{3,2,1,0:T(8,128)(2,1)S(1)}, u32[]{:S(2)}, u32[]{:S(2)}) %collective-permute-start.6) | collective-permute-done | bytes 131104 | tf_op jit(solution)/shard_map/ppermute | solution.py:23
  70.1 4.4 %collective-permute-done.7 = bf16[4,1,128,128]{3,2,1,0:T(8,128)(2,1)S(1)} collective-permute-done((bf16[4,1,128,128]{3,2,1,0:T(8,128)(2,1)S(1)}, bf16[4,1,128,128]{3,2,1,0:T(8,128)(2,1)S(1)}, u32[]{:S(2)}, u32[]{:S(2)}) %collective-permute-start.7) | collective-permute-done | bytes 131104 | tf_op jit(solution)/shard_map/ppermute | solution.py:26
  74.5 1.3 %collective-permute-start.8 = (bf16[4,6,1,128]{3,2,1,0:T(2,128)(2,1)S(1)}, bf16[4,6,1,128]{3,2,1,0:T(2,128)(2,1)S(1)}, u32[]{:S(2)}, u32[]{:S(2)}) collective-permute-start(bf16[4,6,1,128]{3,2,1,0:T(2,128)(2,1)S(1)} %get-tuple-element.47), channel_id=1, source_target_pairs={{0,2},{1,3},{4,6},{5,7},{8,10},{9,11},{12,14},{13,15},{16,18},{17,... | collective-permute-start | bytes 18440 | tf_op jit(solution)/shard_map/ppermute | solution.py:23
  75.8 1.5 %collective-permute-start.9 = (bf16[4,6,1,128]{3,2,1,0:T(2,128)(2,1)S(1)}, bf16[4,6,1,128]{3,2,1,0:T(2,128)(2,1)S(1)}, u32[]{:S(2)}, u32[]{:S(2)}) collective-permute-start(bf16[4,6,1,128]{3,2,1,0:T(2,128)(2,1)S(1)} %get-tuple-element.48), channel_id=1, source_target_pairs={{2,0},{3,1},{6,4},{7,5},{10,8},{11,9},{14,12},{15,13},{18,16},{19,... | collective-permute-start | bytes 18440 | tf_op jit(solution)/shard_map/ppermute | solution.py:26
  77.4 0.1 fusion.20
  77.5 0.1 fusion.21
  77.7 1.2 %collective-permute-done.9 = bf16[4,6,1,128]{3,2,1,0:T(2,128)(2,1)S(1)} collective-permute-done((bf16[4,6,1,128]{3,2,1,0:T(2,128)(2,1)S(1)}, bf16[4,6,1,128]{3,2,1,0:T(2,128)(2,1)S(1)}, u32[]{:S(2)}, u32[]{:S(2)}) %collective-permute-start.9) | collective-permute-done | bytes 6176 | tf_op jit(solution)/shard_map/ppermute | solution.py:26
  78.9 0.5 maximum_maximum_fusion.1
  79.3 0.6 fusion.16
  79.9 0.6 fusion.17
  80.7 1.0 %copy-done.2 = bf16[3,3,3,128,128]{4,3,2,1,0:T(8,128)(2,1)S(1)} copy-done((bf16[3,3,3,128,128]{4,3,2,1,0:T(8,128)(2,1)S(1)}, bf16[3,3,3,128,128]{4,3,2,1,0:T(8,128)(2,1)}, u32[]{:S(2)}) %copy-start.2) | copy-done | bytes 884760
  81.7 0.4 convolution_add_fusion.8
  82.1 0.4 pad_maximum_fusion.18
  82.4 0.4 convolution_add_fusion.7
  82.9 0.4 convolution_add_fusion.6
  83.4 0.4 convolution_add_fusion.5
  83.8 0.4 convolution_add_fusion.4
  84.3 0.4 convolution_add_fusion.3
  84.8 0.4 convolution_add_fusion.2
  85.2 0.4 convolution_add_fusion.1
  85.5 0.1 pad_maximum_fusion.19
  85.7 0.4 convolution_add_fusion
  86.0 0.6 copy-done
  86.6 0.8 fusion.14
  (52 shorter events, 2.6 us)
Async XLA Ops:
  0.0 24.9 %copy-start.3 = (bf16[2,4,128,128]{3,2,1,0:T(8,128)(2,1)S(1)}, bf16[2,4,128,128]{3,2,1,0:T(8,128)(2,1)}, u32[]{:S(2)}) copy-start(bf16[2,4,128,128]{3,2,1,0:T(8,128)(2,1)} %param.12) | copy-start | bytes 786436
  16.9 8.0 %collective-permute-start = (bf16[2,4,128,128]{3,2,1,0:T(8,128)(2,1)S(1)}, bf16[2,4,128,128]{3,2,1,0:T(8,128)(2,1)S(1)}, u32[]{:S(2)}, u32[]{:S(2)}) collective-permute-start(bf16[2,4,128,128]{3,2,1,0:T(8,128)(2,1)S(1)} %fusion.13), channel_id=1, source_target_pairs={{0,1},{2,3},{4,5},{6,7},{8,9},{10,11},{12,13},{14,15},{16,17},{18,... | collective-permute-start | bytes 786440 | tf_op jit(solution)/shard_map/ppermute | solution.py:15
  25.0 5.0 %collective-permute-start.1 = (bf16[4,1,128,128]{3,2,1,0:T(8,128)(2,1)S(1)}, bf16[4,1,128,128]{3,2,1,0:T(8,128)(2,1)S(1)}, u32[]{:S(2)}, u32[]{:S(2)}) collective-permute-start(bf16[4,1,128,128]{3,2,1,0:T(8,128)(2,1)S(1)} %get-tuple-element.71), channel_id=1, source_target_pairs={{0,4},{4,8},{8,12},{1,5},{5,9},{9,13},{2,6},{6,10},{10,14},{3,7},{... | collective-permute-start | bytes 393224 | tf_op jit(solution)/shard_map/ppermute | solution.py:23
  27.5 6.9 %collective-permute-start.2 = (bf16[4,1,128,128]{3,2,1,0:T(8,128)(2,1)S(1)}, bf16[4,1,128,128]{3,2,1,0:T(8,128)(2,1)S(1)}, u32[]{:S(2)}, u32[]{:S(2)}) collective-permute-start(bf16[4,1,128,128]{3,2,1,0:T(8,128)(2,1)S(1)} %get-tuple-element.72), channel_id=1, source_target_pairs={{4,0},{8,4},{12,8},{5,1},{9,5},{13,9},{6,2},{10,6},{14,10},{7,3},{... | collective-permute-start | bytes 393224 | tf_op jit(solution)/shard_map/ppermute | solution.py:26
  34.4 3.0 %collective-permute-start.3 = (bf16[4,6,1,128]{3,2,1,0:T(2,128)(2,1)S(1)}, bf16[4,6,1,128]{3,2,1,0:T(2,128)(2,1)S(1)}, u32[]{:S(2)}, u32[]{:S(2)}) collective-permute-start(bf16[4,6,1,128]{3,2,1,0:T(2,128)(2,1)S(1)} %get-tuple-element.51), channel_id=1, source_target_pairs={{0,2},{1,3},{4,6},{5,7},{8,10},{9,11},{12,14},{13,15},{16,18},{17,... | collective-permute-start | bytes 18440 | tf_op jit(solution)/shard_map/ppermute | solution.py:23
  35.7 3.1 %collective-permute-start.4 = (bf16[4,6,1,128]{3,2,1,0:T(2,128)(2,1)S(1)}, bf16[4,6,1,128]{3,2,1,0:T(2,128)(2,1)S(1)}, u32[]{:S(2)}, u32[]{:S(2)}) collective-permute-start(bf16[4,6,1,128]{3,2,1,0:T(2,128)(2,1)S(1)} %get-tuple-element.52), channel_id=1, source_target_pairs={{2,0},{3,1},{6,4},{7,5},{10,8},{11,9},{14,12},{15,13},{18,16},{19,... | collective-permute-start | bytes 18440 | tf_op jit(solution)/shard_map/ppermute | solution.py:26
  40.2 1.2 %copy-start.1 = (bf16[3,3,3,128,128]{4,3,2,1,0:T(8,128)(2,1)S(1)}, bf16[3,3,3,128,128]{4,3,2,1,0:T(8,128)(2,1)}, u32[]{:S(2)}) copy-start(bf16[3,3,3,128,128]{4,3,2,1,0:T(8,128)(2,1)} %param.16) | copy-start | bytes 2654212
  40.2 1.2 %copy-start.5 = (f32[128]{0:T(128)S(1)}, f32[128]{0:T(128)}, u32[]{:S(2)}) copy-start(f32[128]{0:T(128)} %param.17) | copy-start | bytes 1540
  45.3 11.5 %copy-start.7 = (f32[128]{0:T(128)S(1)}, f32[128]{0:T(128)}, u32[]{:S(2)}) copy-start(f32[128]{0:T(128)} %param.19) | copy-start | bytes 1540
  45.3 11.5 %copy-start.8 = (f32[128]{0:T(128)S(1)}, f32[128]{0:T(128)}, u32[]{:S(2)}) copy-start(f32[128]{0:T(128)} %param.18) | copy-start | bytes 1540
  45.7 19.3 %copy-start.4 = (bf16[2,4,128,128]{3,2,1,0:T(8,128)(2,1)S(1)}, bf16[2,4,128,128]{3,2,1,0:T(8,128)(2,1)}, u32[]{:S(2)}) copy-start(bf16[2,4,128,128]{3,2,1,0:T(8,128)(2,1)} %param.13) | copy-start | bytes 786436
  57.0 8.0 %collective-permute-start.5 = (bf16[2,4,128,128]{3,2,1,0:T(8,128)(2,1)S(1)}, bf16[2,4,128,128]{3,2,1,0:T(8,128)(2,1)S(1)}, u32[]{:S(2)}, u32[]{:S(2)}) collective-permute-start(bf16[2,4,128,128]{3,2,1,0:T(8,128)(2,1)S(1)} %multiply_convert_fusion), channel_id=1, source_target_pairs={{0,1},{2,3},{4,5},{6,7},{8,9},{10,11},{12,13},{14,15},{16,17},{18,... | collective-permute-start | bytes 786440 | tf_op jit(solution)/shard_map/ppermute | solution.py:15
  65.1 5.0 %collective-permute-start.6 = (bf16[4,1,128,128]{3,2,1,0:T(8,128)(2,1)S(1)}, bf16[4,1,128,128]{3,2,1,0:T(8,128)(2,1)S(1)}, u32[]{:S(2)}, u32[]{:S(2)}) collective-permute-start(bf16[4,1,128,128]{3,2,1,0:T(8,128)(2,1)S(1)} %get-tuple-element.67), channel_id=1, source_target_pairs={{0,4},{4,8},{8,12},{1,5},{5,9},{9,13},{2,6},{6,10},{10,14},{3,7},{... | collective-permute-start | bytes 393224 | tf_op jit(solution)/shard_map/ppermute | solution.py:23
  67.6 6.9 %collective-permute-start.7 = (bf16[4,1,128,128]{3,2,1,0:T(8,128)(2,1)S(1)}, bf16[4,1,128,128]{3,2,1,0:T(8,128)(2,1)S(1)}, u32[]{:S(2)}, u32[]{:S(2)}) collective-permute-start(bf16[4,1,128,128]{3,2,1,0:T(8,128)(2,1)S(1)} %get-tuple-element.68), channel_id=1, source_target_pairs={{4,0},{8,4},{12,8},{5,1},{9,5},{13,9},{6,2},{10,6},{14,10},{7,3},{... | collective-permute-start | bytes 393224 | tf_op jit(solution)/shard_map/ppermute | solution.py:26
  74.5 3.2 %collective-permute-start.8 = (bf16[4,6,1,128]{3,2,1,0:T(2,128)(2,1)S(1)}, bf16[4,6,1,128]{3,2,1,0:T(2,128)(2,1)S(1)}, u32[]{:S(2)}, u32[]{:S(2)}) collective-permute-start(bf16[4,6,1,128]{3,2,1,0:T(2,128)(2,1)S(1)} %get-tuple-element.47), channel_id=1, source_target_pairs={{0,2},{1,3},{4,6},{5,7},{8,10},{9,11},{12,14},{13,15},{16,18},{17,... | collective-permute-start | bytes 18440 | tf_op jit(solution)/shard_map/ppermute | solution.py:23
  75.8 3.1 %collective-permute-start.9 = (bf16[4,6,1,128]{3,2,1,0:T(2,128)(2,1)S(1)}, bf16[4,6,1,128]{3,2,1,0:T(2,128)(2,1)S(1)}, u32[]{:S(2)}, u32[]{:S(2)}) collective-permute-start(bf16[4,6,1,128]{3,2,1,0:T(2,128)(2,1)S(1)} %get-tuple-element.48), channel_id=1, source_target_pairs={{2,0},{3,1},{6,4},{7,5},{10,8},{11,9},{14,12},{15,13},{18,16},{19,... | collective-permute-start | bytes 18440 | tf_op jit(solution)/shard_map/ppermute | solution.py:26
  80.5 1.2 %copy-start.2 = (bf16[3,3,3,128,128]{4,3,2,1,0:T(8,128)(2,1)S(1)}, bf16[3,3,3,128,128]{4,3,2,1,0:T(8,128)(2,1)}, u32[]{:S(2)}) copy-start(bf16[3,3,3,128,128]{4,3,2,1,0:T(8,128)(2,1)} %param.20) | copy-start | bytes 2654212
  80.5 1.2 %copy-start.6 = (f32[128]{0:T(128)S(1)}, f32[128]{0:T(128)}, u32[]{:S(2)}) copy-start(f32[128]{0:T(128)} %param.21) | copy-start | bytes 1540
  85.6 1.0 %copy-start = (bf16[2,4,128,128]{3,2,1,0:T(8,128)(2,1)S(1)}, bf16[2,4,128,128]{3,2,1,0:T(8,128)(2,1)}, u32[]{:S(2)}) copy-start(bf16[2,4,128,128]{3,2,1,0:T(8,128)(2,1)} %param.11) | copy-start | bytes 786436

commit v2 on v0

v2 whole, which is shorter than its diff:
```python
import functools

import jax
import jax.numpy as jnp
from jax import lax
from jax.experimental import pallas as pl
from jax.experimental.pallas import tpu as pltpu
from jax.sharding import PartitionSpec as P

G = 32
EPS = 1e-06
BANDS = ("ha", "wa", "ta")
VMEM = pl.BlockSpec(memory_space=pltpu.VMEM)
PAD = 8


def spread_sums(sums):
    count = lax.axis_size("ha") * lax.axis_size("wa") * lax.axis_size("ta")
    copies = jnp.broadcast_to(sums[None], (count, sums.shape[0]))
    return lax.all_to_all(copies, BANDS, 0, 0, tiled=True)


def across(value):
    return lax.ppermute(value, "wa", [(0, 1), (1, 0)])


def row_pairs(later):
    bands, times = lax.axis_size("ha"), lax.axis_size("ta")
    pairs = []
    for band in range(bands):
        for time in range(times - later):
            for core, target in ((0, band - 1), (1, band + 1)):
                if 0 <= target < bands:
                    pairs.append(
                        (
                            (band * 2 + core) * times + time,
                            (target * 2 + 1 - core) * times + time + later,
                        )
                    )
    return pairs


def group_total(value):
    lane = lax.broadcasted_iota(jnp.int32, value.shape, 1)
    chans = value.shape[1]
    pair = value + jnp.where(
        lane % 2 == 0, pltpu.roll(value, chans - 1, 1), pltpu.roll(value, 1, 1)
    )
    return pair + jnp.where(
        lane % 4 < 2, pltpu.roll(pair, chans - 2, 1), pltpu.roll(pair, 2, 1)
    )


def norm_terms(stats_ref, gain_ref, shift_ref, count):
    chans = gain_ref.shape[1]
    total = jnp.sum(stats_ref[...], axis=0, keepdims=True)
    both = jnp.concatenate([total[:, :chans], total[:, chans:]], axis=0)
    both = group_total(jnp.broadcast_to(both[:, None], (2, 8, chans)).reshape(16, chans))
    mean = both[:1] / count
    inverse = lax.rsqrt(both[8:9] / count - mean * mean + EPS)
    return mean, inverse * gain_ref[...] * 0.5, shift_ref[...] * 0.5


def activated(value, terms):
    mean, scale, shift = terms
    half = (value - mean) * scale + shift
    return half + half * jnp.tanh(half)


def pair_weights(w_ref, pair_ref):
    depth, chans = w_ref.shape[1:]
    for tap in range(3):
        for row in range(4):
            for side in range(2):
                at = pair_ref.at[tap * 4 + row, :, pl.ds(side * chans, chans)]
                if 0 <= row - side < 3:
                    at[...] = w_ref[tap * 3 + row - side]
                else:
                    at[...] = jnp.zeros((depth, chans), w_ref.dtype)


def put_row(slab_ref, stage_ref, slot, row, frame):
    cols, chans = slab_ref.shape[2], slab_ref.shape[3] // 3
    for tap in range(3):
        slab_ref[row, frame, :, tap * chans : (tap + 1) * chans] = stage_ref[
            slot, PAD - 1 + tap : PAD - 1 + tap + cols, :
        ].astype(jnp.bfloat16)


def put_halves(slab_ref, stage_ref, slot, core, row, frame, mine, other):
    half = mine.shape[0]
    stage_ref[slot, pl.ds(pl.multiple_of(PAD + core * half, PAD), half), :] = mine
    stage_ref[slot, pl.ds(pl.multiple_of(PAD + (1 - core) * half, PAD), half), :] = other
    put_row(slab_ref, stage_ref, slot, row, frame)


def clear_row(slab_ref, row, frame):
    slab_ref[row, frame] = jnp.zeros(slab_ref.shape[2:], slab_ref.dtype)


def outside(core):
    band = lax.axis_index("ha")
    return band == (lax.axis_size("ha") - 1) * core


def put_block(slab_ref, stage_ref, core, first, mine_ref, other_ref, edge_ref, at, apply):
    for frame in range(2):
        for inner in range(3):
            put_halves(
                slab_ref, stage_ref, (frame * 3 + inner) % 2, core, inner + 1 - core, first + frame,
                apply(mine_ref[frame, inner + core].astype(jnp.float32)),
                apply(other_ref[frame, inner + core].astype(jnp.float32)),
            )
        put_halves(
            slab_ref, stage_ref, frame % 2, core, 3 * core, first + frame,
            apply(edge_ref[at + 2 + frame].astype(jnp.float32)),
            apply(edge_ref[at + frame].astype(jnp.float32)),
        )


def convolve(slab_ref, pair_ref, acc_ref, nout):
    cols, chans = slab_ref.shape[2], slab_ref.shape[3] // 3
    for tap in range(3):
        for row in range(4):
            part = jnp.dot(
                slab_ref[row, tap : tap + nout].reshape(nout * cols, 3 * chans),
                pair_ref[tap * 4 + row],
                preferred_element_type=jnp.float32,
            )
            if tap == 0 and row == 0:
                acc_ref[...] = part
            else:
                acc_ref[...] += part


def clear_pads(stage_ref):
    depth = stage_ref.shape[1]
    for slot in range(stage_ref.shape[0]):
        for start in (0, depth - PAD):
            stage_ref[slot, start : start + PAD, :] = jnp.zeros(
                (PAD, stage_ref.shape[2]), stage_ref.dtype
            )


def first_kernel(count, far, *refs):
    (stats_ref, gain_ref, shift_ref, bias_ref, w_ref, fm, fo, cm, co, pm, po, edge, cedge, *rest) = refs
    if far:
        dm, do, dedge, *rest = rest
    outer_ref, inner_ref, sums_ref, slab_ref, stage_ref, pair_ref, acc_ref = rest
    core, time = lax.axis_index("wa"), lax.axis_index("ta")
    chans = gain_ref.shape[1]
    cols = slab_ref.shape[2]
    pair_weights(w_ref, pair_ref)
    clear_pads(stage_ref)
    terms = norm_terms(stats_ref, gain_ref, shift_ref, count)
    act = functools.partial(activated, terms=terms)
    put = functools.partial(put_block, slab_ref, stage_ref, core)
    put(4, fm, fo, edge, 0, act)

    @pl.when(time == 0)
    def _():
        put(2, pm, po, edge, 4, lambda value: value)

    @pl.when(time > 0)
    def _():
        put(2, cm, co, cedge, 0, act)

    if far:

        @pl.when(time > 1)
        def _():
            put(0, dm, do, dedge, 0, act)

    @pl.when(time <= 1)
    def _():
        put(0, pm, po, edge, 4, lambda value: value)

    @pl.when(outside(core))
    def _():
        for frame in range(6):
            clear_row(slab_ref, 3 * core, frame)

    convolve(slab_ref, pair_ref, acc_ref, 4)
    for row, ref_of in ((0, None), (1, None)):
        value = acc_ref[:, row * chans : (row + 1) * chans] + bias_ref[...]
        own = value[2 * cols :]
        total = jnp.sum(own, axis=0, keepdims=True)
        square = jnp.sum(own * own, axis=0, keepdims=True)
        if row == 0:
            sums_ref[:, :chans] = total
            sums_ref[:, chans:] = square
        else:
            sums_ref[:, :chans] += total
            sums_ref[:, chans:] += square

        @pl.when(core == row)
        def _():
            outer_ref[...] = value.reshape(4, cols, chans)

        @pl.when(core != row)
        def _():
            inner_ref[...] = value.reshape(4, cols, chans)


def second_kernel(count, *refs):
    (stats_ref, gain_ref, shift_ref, bias_ref, w_ref, beyond, outer, inner, near, pm, po, edge, fm, fo) = refs[:14]
    keep_ref, send_ref, slab_ref, stage_ref, pair_ref, acc_ref = refs[14:]
    core, time = lax.axis_index("wa"), lax.axis_index("ta")
    chans = gain_ref.shape[1]
    cols = slab_ref.shape[2]
    half = cols // 2
    pair_weights(w_ref, pair_ref)
    clear_pads(stage_ref)
    terms = norm_terms(stats_ref, gain_ref, shift_ref, count)

    def put_hidden(frame):
        for place, ref in enumerate((beyond, outer, inner, near)):
            slot = place % 2
            stage_ref[slot, PAD : PAD + cols, :] = activated(ref[frame], terms)
            put_row(slab_ref, stage_ref, slot, place + core * (3 - 2 * place), frame)

    put_hidden(2)
    put_hidden(3)

    @pl.when(time == 0)
    def _():
        put_block(slab_ref, stage_ref, core, 0, pm, po, edge, 8, lambda value: value)

    @pl.when(time > 0)
    def _():
        put_hidden(0)
        put_hidden(1)

    @pl.when(outside(core))
    def _():
        for frame in range(4):
            clear_row(slab_ref, 3 * core, frame)

    convolve(slab_ref, pair_ref, acc_ref, 2)
    for frame in range(2):
        for row in range(2):
            for ref, source, side in ((keep_ref, fm, core), (send_ref, fo, 1 - core)):
                start = pl.multiple_of(frame * cols + side * half, half)
                value = acc_ref[pl.ds(start, half), row * chans : (row + 1) * chans] + bias_ref[...]
                value = value + source[frame, row + 2 * core].astype(jnp.float32)
                ref[frame, row] = value.astype(ref.dtype)


def scratch(frames, nout, cols, chans):
    return [
        pltpu.VMEM((4, frames, cols, 3 * chans), jnp.bfloat16),
        pltpu.VMEM((2, cols + 2 * PAD, chans), jnp.float32),
        pltpu.VMEM((12, 3 * chans, 2 * chans), jnp.bfloat16),
        pltpu.VMEM((nout * cols, 2 * chans), jnp.float32),
    ]


def on_device(
    frames,
    past_first,
    past_second,
    gain_first,
    shift_first,
    kernel_first,
    bias_first,
    gain_second,
    shift_second,
    kernel_second,
    bias_second,
):
    nframe, rows, half, chans = frames.shape
    bands, cores, times = (lax.axis_size(axis) for axis in BANDS)
    assert (nframe, rows, cores) == (2, 4, 2)
    cols = 2 * half
    count = float(nframe * rows * half * (chans // G) * bands * cores * times)
    core = lax.axis_index("wa")
    far = times > 2

    def later(value, steps):
        return lax.ppermute(value, "ta", [(i, i + steps) for i in range(times - steps)])

    def flat(vector):
        return vector.reshape(1, -1)

    def stacked(kernel):
        return kernel.reshape(9, 3 * chans, chans)

    carried = later(frames, 1)
    frames_over, first_over, second_over = across(frames), across(past_first), across(past_second)
    outer = jnp.concatenate(
        [
            lax.dynamic_slice_in_dim(value, (rows - 1) * core, 1, 1)[:, 0]
            for value in (frames, frames_over, past_first, first_over, past_second, second_over)
        ]
    )
    edge = lax.ppermute(outer, BANDS, row_pairs(0))
    carried_edge = lax.ppermute(outer[:4], BANDS, row_pairs(1))
    source = frames.astype(jnp.float32)
    sums = jnp.concatenate(
        [jnp.sum(source, axis=(0, 1, 2)), jnp.sum(source * source, axis=(0, 1, 2))]
    )
    gathered = spread_sums(sums)
    behind = [carried, across(carried)]
    operands = [frames, frames_over, *behind, past_first, first_over, edge, carried_edge]
    if far:
        distant = later(frames, 2)
        operands += [distant, across(distant), lax.ppermute(outer[:4], BANDS, row_pairs(2))]
    hidden_row = jax.ShapeDtypeStruct((4, cols, chans), jnp.float32)
    outer_row, inner_row, sums = pl.pallas_call(
        functools.partial(first_kernel, count, far),
        out_shape=(hidden_row, hidden_row, jax.ShapeDtypeStruct((1, 2 * chans), jnp.float32)),
        in_specs=[VMEM] * (5 + len(operands)),
        out_specs=[VMEM] * 3,
        scratch_shapes=scratch(6, 4, cols, chans),
        name="first_conv",
    )(gathered, flat(gain_first), flat(shift_first), flat(bias_first), stacked(kernel_first), *operands)
    beyond_row = lax.ppermute(outer_row, BANDS, row_pairs(0))
    near_row = across(inner_row)
    gathered = spread_sums(sums[0])
    band_half = jax.ShapeDtypeStruct((nframe, 2, half, chans), jnp.bfloat16)
    keep, send = pl.pallas_call(
        functools.partial(second_kernel, count),
        out_shape=(band_half, band_half),
        in_specs=[VMEM] * 14,
        out_specs=[VMEM] * 2,
        scratch_shapes=scratch(4, 2, cols, chans),
        name="second_conv",
    )(
        gathered,
        flat(gain_second),
        flat(shift_second),
        flat(bias_second),
        stacked(kernel_second),
        beyond_row,
        outer_row,
        inner_row,
        near_row,
        past_second,
        second_over,
        edge,
        frames,
        frames_over,
    )
    got = across(send)
    return jnp.where(
        core == 0, jnp.concatenate([keep, got], axis=1), jnp.concatenate([got, keep], axis=1)
    )


def solution(mesh):
    bands = P(("clips", "ta"), "ha", "wa", None)
    past = P("clips", "ha", "wa", None)
    return jax.shard_map(
        on_device,
        mesh=mesh,
        in_specs=(bands, past, past) + (P(),) * 8,
        out_specs=bands,
        check_vma=False,
    )
```

time: 124 us -> 60.6 us (0.49)
  blocking collectives: 67.6 us -> 23.5 us
  waiting for transfers between devices: 21.6 us -> 3.86 us
  Pallas kernels: 0 us -> 14.1 us
  matrix products: 6.64 us -> 0 us
  other arithmetic: 7.01 us -> 1.89 us
  starting transfers between devices: 13.1 us -> 10.1 us
    psum x2 -> x0, blocking collectives: 67.6 us -> none  [the longest x1 34.9 us: on_device(): lax.psum((first_sum, first_square), ('ha', 'wa', 'ta'))]
    all_to_all x0 -> x2, blocking collectives: none -> 23.5 us  [spread_sums(): return lax.all_to_all(copies, BANDS, 0, 0, tiled=True)]
    ppermute x10, waiting for transfers between devices: 21.6 us -> 3.86 us  [the longest x1 2.34 us: later(): lax.ppermute(value, 'ta', [(i, i + steps) for i in range(times - steps)])]
    pallas_call x0 -> x2, Pallas kernels: none -> 14.1 us  [the longest x1 8 us: on_device(): pl.pallas_call(functools.partial(first_kernel, count, far), out_shape=(hi...]
    dot_general x18 -> x0, matrix products: 6.64 us -> none  [conv_block(): jnp.dot(slab.reshape(nframe * out_rows * out_cols, 3 * chans), stacked[ti...]
    unnamed x18 -> x29, local copies, waits for them, and re-layouts: 2.68 us -> 6.48 us
    concatenate x18 -> x2, other arithmetic: 3.1 us -> 0.02 us  [the longest x1 0.01 us: on_device(): jnp.concatenate([lax.dynamic_slice_in_dim(value, (rows - 1) * core, 1, 1)...]
    ppermute x10, starting transfers between devices: 13.1 us -> 10.1 us  [the longest x1 4.39 us: later(): lax.ppermute(value, 'ta', [(i, i + steps) for i in range(times - steps)])]
  transfers between devices with their start and end apart: 10 -> 10, of which waited for: 8 -> 2; matrix products, arithmetic and copies ran while one was open for 1% -> 7% of each run, Pallas kernels for 0% -> 0%
where the time goes in v2:
time: 60.6 us; the launch traced here: 60.1 us
  blocking collectives  23.5 us (39%)
  Pallas kernels  14.1 us (23%)
  starting transfers between devices  10.1 us (17%)
  local copies, waits for them, and re-layouts  6.52 us (11%)
  waiting for transfers between devices  3.86 us (6%)
  other arithmetic  1.89 us (3%)
    all_to_all x2, blocking collectives, spread_sums(): return lax.all_to_all(copies, BANDS, 0, 0, tiled=True)  23.5 us
    pallas_call x1, Pallas kernels, on_device(): pl.pallas_call(functools.partial(first_kernel, count, far), out_shape=(hi...  8 us
    unnamed x29, local copies, waits for them, and re-layouts  6.48 us
    pallas_call x1, Pallas kernels, on_device(): pl.pallas_call(functools.partial(second_kernel, count), out_shape=(band_h...  6.09 us
    ppermute x1, starting transfers between devices, later(): lax.ppermute(value, 'ta', [(i, i + steps) for i in range(times - steps)])  4.39 us
    ppermute x6, starting transfers between devices, across(): return lax.ppermute(value, 'wa', [(0, 1), (1, 0)])  3.66 us
    ppermute x1, waiting for transfers between devices, later(): lax.ppermute(value, 'ta', [(i, i + steps) for i in range(times - steps)])  2.34 us
    select_n x1, other arithmetic, on_device(): jnp.where(core == 0, jnp.concatenate([keep, got], axis=1), jnp.concatenat...  1.72 us
  transfers between devices with their start and end apart: 10, of which 2 were waited for; matrix products, arithmetic and copies ran while one was open for 7% of the time, Pallas kernels for 0%

profile of v2, /device:TPU:0, one launch (start us, length us, event | category | flops | bytes accessed | tf_op | source)
XLA Modules:
  0.0 60.1 jit_solution(16530653415114430673)
XLA Ops:
  0.0 0.5 collective-permute-start
  0.5 4.4 %collective-permute-start.1 = (bf16[2,4,128,128]{3,2,1,0:T(8,128)(2,1)}, bf16[2,4,128,128]{3,2,1,0:T(8,128)(2,1)S(1)}, u32[]{:S(2)}, u32[]{:S(2)}) collective-permute-start(bf16[2,4,128,128]{3,2,1,0:T(8,128)(2,1)} %refs_12_.1), channel_id=1, source_target_pairs={{0,1},{2,3},{4,5},{6,7},{8,9},{10,11},{12,13},{14,15},{16,17},{18,... | collective-permute-start | bytes 786440 | tf_op jit(solution)/shard_map/ppermute | solution.py:280
  4.9 0.3 collective-permute-start.3
  5.2 0.3 collective-permute-start.4
  5.5 0.9 %constant_dynamic-update-slice_fusion.1 = (bf16[12,128,128]{2,1,0:T(8,128)(2,1)S(1)}, bf16[2,128,128]{2,1,0:T(8,128)(2,1)S(1)}) fusion(bf16[2,4,128,128]{3,2,1,0:T(8,128)(2,1)} %refs_12_.1, s32[]{:T(128)S(6)} %select_n.17), kind=kLoop, calls=%fused_computation.14 | loop fusion | bytes 196612
  6.3 0.0 collective-permute-done.refs_6_.refs_13_
  6.3 0.0 copy-start.2
  6.4 0.0 copy-start
  6.4 0.9 %bitcast_dynamic-update-slice_fusion.3 = bf16[12,128,128]{2,1,0:T(8,128)(2,1)S(1)} fusion(bf16[12,128,128]{2,1,0:T(8,128)(2,1)S(1)} %get-tuple-element.17, bf16[2,4,128,128]{3,2,1,0:T(8,128)(2,1)} %refs_9_.2, s32[]{:T(128)S(6)} %select_n.17), kind=kLoop, calls=%fused_computation.8 | loop fusion | bytes 131076
  7.3 0.0 collective-permute-done.3.refs_10_
  7.4 0.0 copy-start.6
  7.4 0.9 %bitcast_dynamic-update-slice_fusion.1 = bf16[12,128,128]{2,1,0:T(8,128)(2,1)S(1)} fusion(bf16[12,128,128]{2,1,0:T(8,128)(2,1)S(1)} %bitcast_dynamic-update-slice_fusion.2, bf16[2,4,128,128]{3,2,1,0:T(8,128)(2,1)} %refs_9_.3, s32[]{:T(128)S(6)} %select_n.17), kind=kLoop, calls=%fused_computation.6 | loop fusion | bytes 131076
  8.3 0.0 copy-done.2
  8.3 0.0 collective-permute-done.4.refs_10_
  8.3 0.0 copy-start.5
  8.4 0.7 %collective-permute-start.5 = (bf16[12,128,128]{2,1,0:T(8,128)(2,1)S(1)}, bf16[12,128,128]{2,1,0:T(8,128)(2,1)S(1)}, u32[]{:S(2)}, u32[]{:S(2)}) collective-permute-start(bf16[12,128,128]{2,1,0:T(8,128)(2,1)S(1)} %bitcast_dynamic-update-slice_fusion), channel_id=1, source_target_pairs={{2,4},{3,5},{4,2},{6,8},{5,3},{7,9},{8,6},{10,12},{9,7},{11,13},{1... | collective-permute-start | bytes 1179656 | tf_op jit(solution)/shard_map/ppermute | solution.py:296
  9.1 2.3 %collective-permute-done.1.refs_7_ = bf16[2,4,128,128]{3,2,1,0:T(8,128)(2,1)S(1)} collective-permute-done((bf16[2,4,128,128]{3,2,1,0:T(8,128)(2,1)}, bf16[2,4,128,128]{3,2,1,0:T(8,128)(2,1)S(1)}, u32[]{:S(2)}, u32[]{:S(2)}) %collective-permute-start.1) | collective-permute-done | bytes 262176 | tf_op jit(solution)/shard_map/ppermute | solution.py:280
  11.4 0.0 copy-start.7
  11.4 0.7 %collective-permute-start.2 = (bf16[2,4,128,128]{3,2,1,0:T(8,128)(2,1)S(1)}, bf16[2,4,128,128]{3,2,1,0:T(8,128)(2,1)S(1)}, u32[]{:S(2)}, u32[]{:S(2)}) collective-permute-start(bf16[2,4,128,128]{3,2,1,0:T(8,128)(2,1)S(1)} %collective-permute-done.1.refs_7_), channel_id=1, source_target_pairs={{0,2},{2,0},{1,3},{3,1},{4,6},{6,4},{5,7},{7,5},{8,10},{10,8},{9,1... | collective-permute-start | bytes 786440 | tf_op jit(solution)/shard_map/ppermute | solution.py:24
  12.1 0.0 copy-done
  12.1 0.2 convert_reduce_fusion
  12.2 0.0 copy-done.6
  12.2 0.0 copy-done.5
  12.3 0.0 copy-done.7
  12.3 0.7 %collective-permute-start.6 = (bf16[4,128,128]{2,1,0:T(8,128)(2,1)S(1)}, bf16[4,128,128]{2,1,0:T(8,128)(2,1)S(1)}, u32[]{:S(2)}, u32[]{:S(2)}) collective-permute-start(bf16[4,128,128]{2,1,0:T(8,128)(2,1)S(1)} %pad_maximum_fusion), channel_id=1, source_target_pairs={{2,5},{4,3},{6,9},{8,7},{10,13},{12,11},{18,21},{20,19},{22,25},{2... | collective-permute-start | bytes 393224 | tf_op jit(solution)/shard_map/ppermute | solution.py:297
  13.0 14.4 %all_to_all.16 = f32[16,1,256]{2,1,0:T(1,128)S(1)} all-to-all(f32[16,1,256]{2,1,0:T(1,128)S(1)} %broadcast_in_dim.4), channel_id=1, replica_groups=mesh['clips'=2,'ha'=4,'wa'=2,'ta'=2] {'ha','wa','ta'}, dimensions={0} | all-to-all | bytes 32768 | tf_op jit(solution)/shard_map/all_to_all | solution.py:20
  27.4 0.6 copy.17
  28.0 0.0 collective-permute-done.6.refs_12_
  28.0 0.0 copy-start.9
  28.0 0.0 collective-permute-done.2.refs_8_
  28.0 0.0 copy-start.8
  28.0 0.0 collective-permute-done.5.refs_11_
  28.0 0.0 copy-start.1
  28.0 0.6 %copy-done.9 = bf16[4,128,128]{2,1,0:T(8,128)(2,1)} copy-done((bf16[4,128,128]{2,1,0:T(8,128)(2,1)}, bf16[4,128,128]{2,1,0:T(8,128)(2,1)S(1)}, u32[]{:S(2)}) %copy-start.9) | copy-done | bytes 131096
  28.6 0.1 copy-done.8
  28.7 0.2 copy-done.1
  28.9 8.0 %first_conv.1 = (f32[4,256,128]{2,1,0:T(8,128)}, f32[4,256,128]{2,1,0:T(8,128)}, f32[1,256]{1,0:T(1,128)}) custom-call(f32[16,256]{1,0:T(8,128)} %bitcast.31, f32[1,128]{1,0:T(1,128)} %bitcast.34, f32[1,128]{1,0:T(1,128)} %bitcast.35, f32[1,128]{1,0:T(1,128)} %bitcast.36, bf16[9,384,128]{2,1,0:T(8,128)(2,1)} %bitcast.29, bf16[2,4,128,128]{3,2,1,0:T(8,128)(2,1)} %refs_12_.1, ...), custom_call_target="tpu_custom_call" | custom-call | tf_op jit(solution)/shard_map/first_conv/pallas_call | solution.py:309
  36.9 0.7 %collective-permute-start.7 = (f32[4,256,128]{2,1,0:T(8,128)}, f32[4,256,128]{2,1,0:T(8,128)S(1)}, u32[]{:S(2)}, u32[]{:S(2)}) collective-permute-start(f32[4,256,128]{2,1,0:T(8,128)} %get-tuple-element.11.refs_6_), channel_id=1, source_target_pairs={{2,4},{3,5},{4,2},{6,8},{5,3},{7,9},{8,6},{10,12},{9,7},{11,13},{1... | collective-permute-start | bytes 1572872 | tf_op jit(solution)/shard_map/ppermute | solution.py:317
  37.6 1.9 %collective-permute-start.8 = (f32[4,256,128]{2,1,0:T(8,128)}, f32[4,256,128]{2,1,0:T(8,128)S(1)}, u32[]{:S(2)}, u32[]{:S(2)}) collective-permute-start(f32[4,256,128]{2,1,0:T(8,128)} %get-tuple-element.12.refs_7_), channel_id=1, source_target_pairs={{0,2},{2,0},{1,3},{3,1},{4,6},{6,4},{5,7},{7,5},{8,10},{10,8},{9,1... | collective-permute-start | bytes 1572872 | tf_op jit(solution)/shard_map/ppermute | solution.py:24
  39.5 0.0 copy-start.10
  39.5 0.6 %copy-done.10 = f32[1,256]{1,0:T(1,128)S(1)} copy-done((f32[1,256]{1,0:T(1,128)S(1)}, f32[1,256]{1,0:T(1,128)}, u32[]{:S(2)}) %copy-start.10) | copy-done | bytes 1048
  40.1 9.1 %all_to_all.17 = f32[16,1,256]{2,1,0:T(1,128)S(1)} all-to-all(f32[16,1,256]{2,1,0:T(1,128)S(1)} %broadcast_in_dim.5), channel_id=1, replica_groups=mesh['clips'=2,'ha'=4,'wa'=2,'ta'=2] {'ha','wa','ta'}, dimensions={0} | all-to-all | bytes 32768 | tf_op jit(solution)/shard_map/all_to_all | solution.py:20
  49.2 0.6 %copy.16 = f32[16,1,256]{2,0,1:T(8,128)} copy(f32[16,1,256]{2,1,0:T(1,128)S(1)} %all_to_all.17) | data formatting | bytes 32768
  49.8 0.0 collective-permute-done.7.refs_5_
  49.8 0.0 copy-start.3
  49.8 0.0 collective-permute-done.8.refs_8_
  49.8 0.0 copy-start.4
  49.8 0.8 %copy-done.3 = f32[4,256,128]{2,1,0:T(8,128)} copy-done((f32[4,256,128]{2,1,0:T(8,128)}, f32[4,256,128]{2,1,0:T(8,128)S(1)}, u32[]{:S(2)}) %copy-start.3) | copy-done | bytes 524312
  50.6 0.2 copy-done.4
  50.8 6.1 %second_conv.1 = (bf16[2,2,128,128]{3,2,1,0:T(8,128)(2,1)}, bf16[2,2,128,128]{3,2,1,0:T(8,128)(2,1)}) custom-call(f32[16,256]{1,0:T(8,128)} %bitcast.32, f32[1,128]{1,0:T(1,128)} %bitcast.37, f32[1,128]{1,0:T(1,128)} %bitcast.38, f32[1,128]{1,0:T(1,128)} %bitcast.39, bf16[9,384,128]{2,1,0:T(8,128)(2,1)} %bitcast.30, f32[4,256,128]{2,1,0:T(8,128)} %copy-done.3, ...), custom_call_target="tpu_custom_call" | custom-call | tf_op jit(solution)/shard_map/second_conv/pallas_call | solution.py:321
  56.9 0.1 collective-permute-start.9
  56.9 1.5 %collective-permute-done.9 = bf16[2,2,128,128]{3,2,1,0:T(8,128)(2,1)S(1)} collective-permute-done((bf16[2,2,128,128]{3,2,1,0:T(8,128)(2,1)}, bf16[2,2,128,128]{3,2,1,0:T(8,128)(2,1)S(1)}, u32[]{:S(2)}, u32[]{:S(2)}) %collective-permute-start.9) | collective-permute-done | bytes 131104 | tf_op jit(solution)/shard_map/ppermute | solution.py:24
  58.4 1.7 %maximum_select_fusion = bf16[2,4,128,128]{3,2,1,0:T(8,128)(2,1)} fusion(bf16[2,2,128,128]{3,2,1,0:T(8,128)(2,1)S(1)} %collective-permute-done.9, bf16[2,2,128,128]{3,2,1,0:T(8,128)(2,1)} %get-tuple-element.13, pred[]{:T(512)S(6)} %eq.3), kind=kLoop, calls=%fused_computation.3 | loop fusion | flops 393216 | bytes 524289 | tf_op jit(solution)/shard_map/jit(_where)/select_n | solution.py:345
  (7 shorter events, 0.1 us)
Async XLA Ops:
  0.0 6.3 %collective-permute-start = (bf16[2,4,128,128]{3,2,1,0:T(8,128)(2,1)}, bf16[2,4,128,128]{3,2,1,0:T(8,128)(2,1)S(1)}, u32[]{:S(2)}, u32[]{:S(2)}) collective-permute-start(bf16[2,4,128,128]{3,2,1,0:T(8,128)(2,1)} %refs_12_.1), channel_id=1, source_target_pairs={{0,2},{2,0},{1,3},{3,1},{4,6},{6,4},{5,7},{7,5},{8,10},{10,8},{9,1... | collective-permute-start | bytes 786440 | tf_op jit(solution)/shard_map/ppermute | solution.py:24
  0.5 10.9 %collective-permute-start.1 = (bf16[2,4,128,128]{3,2,1,0:T(8,128)(2,1)}, bf16[2,4,128,128]{3,2,1,0:T(8,128)(2,1)S(1)}, u32[]{:S(2)}, u32[]{:S(2)}) collective-permute-start(bf16[2,4,128,128]{3,2,1,0:T(8,128)(2,1)} %refs_12_.1), channel_id=1, source_target_pairs={{0,1},{2,3},{4,5},{6,7},{8,9},{10,11},{12,13},{14,15},{16,17},{18,... | collective-permute-start | bytes 786440 | tf_op jit(solution)/shard_map/ppermute | solution.py:280
  4.9 2.5 %collective-permute-start.3 = (bf16[2,4,128,128]{3,2,1,0:T(8,128)(2,1)}, bf16[2,4,128,128]{3,2,1,0:T(8,128)(2,1)S(1)}, u32[]{:S(2)}, u32[]{:S(2)}) collective-permute-start(bf16[2,4,128,128]{3,2,1,0:T(8,128)(2,1)} %refs_9_.2), channel_id=1, source_target_pairs={{0,2},{2,0},{1,3},{3,1},{4,6},{6,4},{5,7},{7,5},{8,10},{10,8},{9,1... | collective-permute-start | bytes 786440 | tf_op jit(solution)/shard_map/ppermute | solution.py:24
  5.2 3.1 %collective-permute-start.4 = (bf16[2,4,128,128]{3,2,1,0:T(8,128)(2,1)}, bf16[2,4,128,128]{3,2,1,0:T(8,128)(2,1)S(1)}, u32[]{:S(2)}, u32[]{:S(2)}) collective-permute-start(bf16[2,4,128,128]{3,2,1,0:T(8,128)(2,1)} %refs_9_.3), channel_id=1, source_target_pairs={{0,2},{2,0},{1,3},{3,1},{4,6},{6,4},{5,7},{7,5},{8,10},{10,8},{9,1... | collective-permute-start | bytes 786440 | tf_op jit(solution)/shard_map/ppermute | solution.py:24
  6.3 2.0 %copy-start.2 = (bf16[2,4,128,128]{3,2,1,0:T(8,128)(2,1)}, bf16[2,4,128,128]{3,2,1,0:T(8,128)(2,1)S(1)}, u32[]{:S(2)}) copy-start(bf16[2,4,128,128]{3,2,1,0:T(8,128)(2,1)S(1)} %collective-permute-done.refs_6_.refs_13_) | copy-start | bytes 786436
  6.4 5.7 %copy-start = (bf16[2,4,128,128]{3,2,1,0:T(8,128)(2,1)S(1)}, bf16[2,4,128,128]{3,2,1,0:T(8,128)(2,1)}, u32[]{:S(2)}) copy-start(bf16[2,4,128,128]{3,2,1,0:T(8,128)(2,1)} %refs_12_.1) | copy-start | bytes 786436
  7.4 4.9 %copy-start.6 = (bf16[2,4,128,128]{3,2,1,0:T(8,128)(2,1)}, bf16[2,4,128,128]{3,2,1,0:T(8,128)(2,1)S(1)}, u32[]{:S(2)}) copy-start(bf16[2,4,128,128]{3,2,1,0:T(8,128)(2,1)S(1)} %collective-permute-done.3.refs_10_) | copy-start | bytes 786436
  8.3 3.9 %copy-start.5 = (bf16[2,4,128,128]{3,2,1,0:T(8,128)(2,1)}, bf16[2,4,128,128]{3,2,1,0:T(8,128)(2,1)S(1)}, u32[]{:S(2)}) copy-start(bf16[2,4,128,128]{3,2,1,0:T(8,128)(2,1)S(1)} %collective-permute-done.4.refs_10_) | copy-start | bytes 786436
  8.4 19.6 %collective-permute-start.5 = (bf16[12,128,128]{2,1,0:T(8,128)(2,1)S(1)}, bf16[12,128,128]{2,1,0:T(8,128)(2,1)S(1)}, u32[]{:S(2)}, u32[]{:S(2)}) collective-permute-start(bf16[12,128,128]{2,1,0:T(8,128)(2,1)S(1)} %bitcast_dynamic-update-slice_fusion), channel_id=1, source_target_pairs={{2,4},{3,5},{4,2},{6,8},{5,3},{7,9},{8,6},{10,12},{9,7},{11,13},{1... | collective-permute-start | bytes 1179656 | tf_op jit(solution)/shard_map/ppermute | solution.py:296
  11.4 0.9 %copy-start.7 = (bf16[2,4,128,128]{3,2,1,0:T(8,128)(2,1)}, bf16[2,4,128,128]{3,2,1,0:T(8,128)(2,1)S(1)}, u32[]{:S(2)}) copy-start(bf16[2,4,128,128]{3,2,1,0:T(8,128)(2,1)S(1)} %collective-permute-done.1.refs_7_) | copy-start | bytes 786436
  11.4 16.6 %collective-permute-start.2 = (bf16[2,4,128,128]{3,2,1,0:T(8,128)(2,1)S(1)}, bf16[2,4,128,128]{3,2,1,0:T(8,128)(2,1)S(1)}, u32[]{:S(2)}, u32[]{:S(2)}) collective-permute-start(bf16[2,4,128,128]{3,2,1,0:T(8,128)(2,1)S(1)} %collective-permute-done.1.refs_7_), channel_id=1, source_target_pairs={{0,2},{2,0},{1,3},{3,1},{4,6},{6,4},{5,7},{7,5},{8,10},{10,8},{9,1... | collective-permute-start | bytes 786440 | tf_op jit(solution)/shard_map/ppermute | solution.py:24
  12.3 15.7 %collective-permute-start.6 = (bf16[4,128,128]{2,1,0:T(8,128)(2,1)S(1)}, bf16[4,128,128]{2,1,0:T(8,128)(2,1)S(1)}, u32[]{:S(2)}, u32[]{:S(2)}) collective-permute-start(bf16[4,128,128]{2,1,0:T(8,128)(2,1)S(1)} %pad_maximum_fusion), channel_id=1, source_target_pairs={{2,5},{4,3},{6,9},{8,7},{10,13},{12,11},{18,21},{20,19},{22,25},{2... | collective-permute-start | bytes 393224 | tf_op jit(solution)/shard_map/ppermute | solution.py:297
  28.0 0.7 %copy-start.9 = (bf16[4,128,128]{2,1,0:T(8,128)(2,1)}, bf16[4,128,128]{2,1,0:T(8,128)(2,1)S(1)}, u32[]{:S(2)}) copy-start(bf16[4,128,128]{2,1,0:T(8,128)(2,1)S(1)} %collective-permute-done.6.refs_12_) | copy-start | bytes 393220
  28.0 0.7 %copy-start.8 = (bf16[2,4,128,128]{3,2,1,0:T(8,128)(2,1)}, bf16[2,4,128,128]{3,2,1,0:T(8,128)(2,1)S(1)}, u32[]{:S(2)}) copy-start(bf16[2,4,128,128]{3,2,1,0:T(8,128)(2,1)S(1)} %collective-permute-done.2.refs_8_) | copy-start | bytes 786436
  28.0 0.9 %copy-start.1 = (bf16[12,128,128]{2,1,0:T(8,128)(2,1)}, bf16[12,128,128]{2,1,0:T(8,128)(2,1)S(1)}, u32[]{:S(2)}) copy-start(bf16[12,128,128]{2,1,0:T(8,128)(2,1)S(1)} %collective-permute-done.5.refs_11_) | copy-start | bytes 1179652
  36.9 12.9 %collective-permute-start.7 = (f32[4,256,128]{2,1,0:T(8,128)}, f32[4,256,128]{2,1,0:T(8,128)S(1)}, u32[]{:S(2)}, u32[]{:S(2)}) collective-permute-start(f32[4,256,128]{2,1,0:T(8,128)} %get-tuple-element.11.refs_6_), channel_id=1, source_target_pairs={{2,4},{3,5},{4,2},{6,8},{5,3},{7,9},{8,6},{10,12},{9,7},{11,13},{1... | collective-permute-start | bytes 1572872 | tf_op jit(solution)/shard_map/ppermute | solution.py:317
  37.6 12.2 %collective-permute-start.8 = (f32[4,256,128]{2,1,0:T(8,128)}, f32[4,256,128]{2,1,0:T(8,128)S(1)}, u32[]{:S(2)}, u32[]{:S(2)}) collective-permute-start(f32[4,256,128]{2,1,0:T(8,128)} %get-tuple-element.12.refs_7_), channel_id=1, source_target_pairs={{0,2},{2,0},{1,3},{3,1},{4,6},{6,4},{5,7},{7,5},{8,10},{10,8},{9,1... | collective-permute-start | bytes 1572872 | tf_op jit(solution)/shard_map/ppermute | solution.py:24
  39.5 0.6 %copy-start.10 = (f32[1,256]{1,0:T(1,128)S(1)}, f32[1,256]{1,0:T(1,128)}, u32[]{:S(2)}) copy-start(f32[1,256]{1,0:T(1,128)} %get-tuple-element.10) | copy-start | bytes 3076
  49.8 0.8 %copy-start.3 = (f32[4,256,128]{2,1,0:T(8,128)}, f32[4,256,128]{2,1,0:T(8,128)S(1)}, u32[]{:S(2)}) copy-start(f32[4,256,128]{2,1,0:T(8,128)S(1)} %collective-permute-done.7.refs_5_) | copy-start | bytes 1572868
  49.8 1.0 %copy-start.4 = (f32[4,256,128]{2,1,0:T(8,128)}, f32[4,256,128]{2,1,0:T(8,128)S(1)}, u32[]{:S(2)}) copy-start(f32[4,256,128]{2,1,0:T(8,128)S(1)} %collective-permute-done.8.refs_8_) | copy-start | bytes 1572868
  56.9 1.6 %collective-permute-start.9 = (bf16[2,2,128,128]{3,2,1,0:T(8,128)(2,1)}, bf16[2,2,128,128]{3,2,1,0:T(8,128)(2,1)S(1)}, u32[]{:S(2)}, u32[]{:S(2)}) collective-permute-start(bf16[2,2,128,128]{3,2,1,0:T(8,128)(2,1)} %get-tuple-element.14), channel_id=1, source_target_pairs={{0,2},{2,0},{1,3},{3,1},{4,6},{6,4},{5,7},{7,5},{8,10},{10,8},{9,1... | collective-permute-start | bytes 393224 | tf_op jit(solution)/shard_map/ppermute | solution.py:24
